TPU v7x, 32 devices: a whole 2x2x4 slice. The times are simulated.
32 devices in a mesh: dp: 8 (over z, x), mx: 2 (over y), my: 2 (over core).
Axes of the slice: x: 2, y: 2, z: 4, core: 2. Of those that a mesh axis runs over, the one named last changes fastest.
Arguments:
- layer_input: bfloat16 [32768, 768], P(('dp', 'mx', 'my')), may hold values from -6 to 6
- w_qkv: bfloat16 [768, 2304], P('mx', 'my'), may hold values from -0.21875 to 0.21875
- b_qkv: bfloat16 [2304], P(('mx', 'my')), may hold values from -3 to 3
- w_out: bfloat16 [768, 768], P('mx', 'my'), may hold values from -0.875 to 0.875
- b_out: bfloat16 [768], P(('mx', 'my')), may hold values from -2 to 2
- ln1_gain: bfloat16 [768], P(('mx', 'my')), may hold values from 0.5 to 1.5
- ln1_bias: bfloat16 [768], P(('mx', 'my')), may hold values from -2 to 2
- w_up: bfloat16 [768, 3072], P('mx', 'my'), may hold values from -0.21875 to 0.21875
- b_up: bfloat16 [3072], P(('mx', 'my')), may hold values from -3 to 3
- w_down: bfloat16 [3072, 768], P('mx', 'my'), may hold values from -0.109375 to 0.109375
- b_down: bfloat16 [768], P(('mx', 'my')), may hold values from -2 to 2
- ln2_gain: bfloat16 [768], P(('mx', 'my')), may hold values from 0.5 to 1.5
- ln2_bias: bfloat16 [768], P(('mx', 'my')), may hold values from -2 to 2
- segment_ids: int32 [32768], P(('dp', 'mx', 'my')), may hold values from 0 to 7, as said below
- doc_lengths: int32 [32, 8], P(('dp', 'mx', 'my')), may hold values from 1 to 1017, as said below
- cotangent: bfloat16 [32768, 768], P(('dp', 'mx', 'my')), may hold values from -6 to 6
Outputs:
- block_out: bfloat16 [32768, 768], P(('dp', 'mx', 'my'))
- input_grad: bfloat16 [32768, 768], P(('dp', 'mx', 'my'))
- grad_w_qkv: float32 [768, 2304], P('mx', 'my')
- grad_b_qkv: float32 [2304], P(('mx', 'my'))
- grad_w_out: float32 [768, 768], P('mx', 'my')
- grad_b_out: float32 [768], P(('mx', 'my'))
- grad_ln1_gain: float32 [768], P(('mx', 'my'))
- grad_ln1_bias: float32 [768], P(('mx', 'my'))
- grad_w_up: float32 [768, 3072], P('mx', 'my')
- grad_b_up: float32 [3072], P(('mx', 'my'))
- grad_w_down: float32 [3072, 768], P('mx', 'my')
- grad_b_down: float32 [768], P(('mx', 'my'))
- grad_ln2_gain: float32 [768], P(('mx', 'my'))
- grad_ln2_bias: float32 [768], P(('mx', 'my'))
Inputs may be any that keep to these rules, and one draw needn't show every extreme that they name: Each sequence of 1024 tokens holds exactly 8 documents back to back; segment_ids starts at 0 at each sequence's first token and rises by one at each document's first token. `doc_lengths`: A sequence's lengths sum to 1024 and are the lengths of its documents in order, as segment_ids lays them out.
All inputs are finite; a program needn't handle non-finite values.
Results may differ from a plain program's by a relative error of at most 0.018.
Values may be sent and summed in bfloat16 or wider, within the bound.
No kernel may reach another device: no remote copies, remote signals or barrier semaphores. Data moves between devices by JAX's collectives and lax.ppermute only.
A program may use at most 192 MiB of HBM per device.

v0:
```python
import math
import jax
import jax.numpy as jnp
from jax import lax
from jax.sharding import PartitionSpec as P

HD = 64
norm_eps = 1e-05


def layer_norm(resid, gain, shift):
    center = resid - jnp.mean(resid, axis=-1, keepdims=True)
    spread = jnp.mean(center * center, axis=-1, keepdims=True)
    return center * lax.rsqrt(spread + norm_eps) * gain + shift


def gelu_exact(values):
    return jax.nn.gelu(values, approximate=False)


def geometry(segment, spans):
    doc_count = spans.shape[0]
    member = segment[:, None] == jnp.arange(doc_count, dtype=jnp.int32)[None, :]
    doc_span = jnp.sum(jnp.where(member, spans[None, :], 0), axis=1)
    length = segment.shape[0]
    places = jnp.arange(length, dtype=jnp.int32)
    angle = 0.5 * math.pi * places.astype(jnp.float32) / doc_span.astype(jnp.float32)
    causal = places[:, None] >= places[None, :]
    keep_mask = jnp.where((segment[:, None] == segment[None, :]) & causal, 1.0, 0.0).astype(
        jnp.float32
    )
    return (jnp.cos(angle), jnp.sin(angle), keep_mask)


def project_forward(operand, matrix):
    rows_here = operand.shape[0]
    grid_rows, grid_cols, row_size, col_size = matrix.shape
    result = jnp.einsum(
        "tid,ijdn->tjn",
        operand.reshape(rows_here, grid_rows, row_size),
        matrix,
        preferred_element_type=jnp.float32,
    )
    return result.reshape(rows_here, grid_cols * col_size)


def project_back(grad_rows, matrix):
    rows_here = grad_rows.shape[0]
    grid_rows, grid_cols, row_size, col_size = matrix.shape
    result = jnp.einsum(
        "tjn,ijdn->tid",
        grad_rows.reshape(rows_here, grid_cols, col_size),
        matrix,
        preferred_element_type=jnp.float32,
    )
    return result.reshape(rows_here, grid_rows * row_size)


def weight_grad(operand, grad_rows, matrix):
    rows_here = operand.shape[0]
    grid_rows, grid_cols, row_size, col_size = matrix.shape
    result = jnp.einsum(
        "tid,tjn->ijdn",
        operand.reshape(rows_here, grid_rows, row_size),
        grad_rows.reshape(rows_here, grid_cols, col_size),
        preferred_element_type=jnp.float32,
    )
    return result.reshape(grid_rows * grid_cols, row_size, col_size)


def fetch_weights(
    w_qkv, w_out, w_up, w_down, b_qkv, b_out, ln1_gain, ln1_bias, b_up, b_down, ln2_gain, ln2_bias
):
    fetched = (
        lax.all_gather(w_qkv[None], ("mx", "my"), axis=0, tiled=True),
        lax.all_gather(w_out[None], ("mx", "my"), axis=0, tiled=True),
        lax.all_gather(w_up[None], ("mx", "my"), axis=0, tiled=True),
        lax.all_gather(w_down[None], ("mx", "my"), axis=0, tiled=True),
        lax.all_gather(b_qkv, ("mx", "my"), axis=0, tiled=True),
        lax.all_gather(b_out, ("mx", "my"), axis=0, tiled=True),
        lax.all_gather(ln1_gain, ("mx", "my"), axis=0, tiled=True),
        lax.all_gather(ln1_bias, ("mx", "my"), axis=0, tiled=True),
        lax.all_gather(b_up, ("mx", "my"), axis=0, tiled=True),
        lax.all_gather(b_down, ("mx", "my"), axis=0, tiled=True),
        lax.all_gather(ln2_gain, ("mx", "my"), axis=0, tiled=True),
        lax.all_gather(ln2_bias, ("mx", "my"), axis=0, tiled=True),
    )
    grid_rows = lax.axis_size("mx")
    grid_cols = lax.axis_size("my")
    matrices = tuple(
        (
            piece.reshape(grid_rows, grid_cols, piece.shape[1], piece.shape[2])
            for piece in fetched[:4]
        )
    )
    return (matrices, fetched[4:], "stack")


def reduce_grads(grads):
    summed = (
        lax.psum_scatter(
            grads[0].astype(jnp.bfloat16), ("mx", "my"), scatter_dimension=0, tiled=True
        ).astype(jnp.float32),
        lax.psum_scatter(
            grads[1].astype(jnp.bfloat16), ("mx", "my"), scatter_dimension=0, tiled=True
        ).astype(jnp.float32),
        lax.psum_scatter(
            grads[2].astype(jnp.bfloat16), ("mx", "my"), scatter_dimension=0, tiled=True
        ).astype(jnp.float32),
        lax.psum_scatter(
            grads[3].astype(jnp.bfloat16), ("mx", "my"), scatter_dimension=0, tiled=True
        ).astype(jnp.float32),
        lax.psum_scatter(
            grads[4].astype(jnp.bfloat16), ("mx", "my"), scatter_dimension=0, tiled=True
        ).astype(jnp.float32),
        lax.psum_scatter(
            grads[5].astype(jnp.bfloat16), ("mx", "my"), scatter_dimension=0, tiled=True
        ).astype(jnp.float32),
        lax.psum_scatter(
            grads[6].astype(jnp.bfloat16), ("mx", "my"), scatter_dimension=0, tiled=True
        ).astype(jnp.float32),
        lax.psum_scatter(
            grads[7].astype(jnp.bfloat16), ("mx", "my"), scatter_dimension=0, tiled=True
        ).astype(jnp.float32),
        lax.psum_scatter(
            grads[8].astype(jnp.bfloat16), ("mx", "my"), scatter_dimension=0, tiled=True
        ).astype(jnp.float32),
        lax.psum_scatter(
            grads[9].astype(jnp.bfloat16), ("mx", "my"), scatter_dimension=0, tiled=True
        ).astype(jnp.float32),
        lax.psum_scatter(
            grads[10].astype(jnp.bfloat16), ("mx", "my"), scatter_dimension=0, tiled=True
        ).astype(jnp.float32),
        lax.psum_scatter(
            grads[11].astype(jnp.bfloat16), ("mx", "my"), scatter_dimension=0, tiled=True
        ).astype(jnp.float32),
    )
    blocks = tuple((piece[0] for piece in summed[:4])) + tuple(summed[4:])
    return (
        lax.psum(blocks[0].astype(jnp.bfloat16), "dp").astype(jnp.float32),
        lax.psum(blocks[1].astype(jnp.bfloat16), "dp").astype(jnp.float32),
        lax.psum(blocks[2].astype(jnp.bfloat16), "dp").astype(jnp.float32),
        lax.psum(blocks[3].astype(jnp.bfloat16), "dp").astype(jnp.float32),
        lax.psum(blocks[4].astype(jnp.bfloat16), "dp").astype(jnp.float32),
        lax.psum(blocks[5].astype(jnp.bfloat16), "dp").astype(jnp.float32),
        lax.psum(blocks[6].astype(jnp.bfloat16), "dp").astype(jnp.float32),
        lax.psum(blocks[7].astype(jnp.bfloat16), "dp").astype(jnp.float32),
        lax.psum(blocks[8].astype(jnp.bfloat16), "dp").astype(jnp.float32),
        lax.psum(blocks[9].astype(jnp.bfloat16), "dp").astype(jnp.float32),
        lax.psum(blocks[10].astype(jnp.bfloat16), "dp").astype(jnp.float32),
        lax.psum(blocks[11].astype(jnp.bfloat16), "dp").astype(jnp.float32),
    )


def body(
    layer_input,
    w_qkv,
    b_qkv,
    w_out,
    b_out,
    ln1_gain,
    ln1_bias,
    w_up,
    b_up,
    w_down,
    b_down,
    ln2_gain,
    ln2_bias,
    segment_ids,
    doc_lengths,
    cotangent,
):
    seqs_here = doc_lengths.shape[0]
    tokens = layer_input.shape[0]
    length = tokens // seqs_here
    model_width = layer_input.shape[1]
    head_count = model_width // HD
    cosine, sine, keep_mask = jax.vmap(geometry)(
        segment_ids.reshape(seqs_here, length), doc_lengths
    )
    cos_col = cosine[:, :, None, None]
    sin_col = sine[:, :, None, None]
    matrices, vectors, layout = fetch_weights(
        w_qkv,
        w_out,
        w_up,
        w_down,
        b_qkv,
        b_out,
        ln1_gain,
        ln1_bias,
        b_up,
        b_down,
        ln2_gain,
        ln2_bias,
    )
    m_qkv, m_out, m_up, m_down = matrices
    f_bqkv, f_bout, f_gain1, f_bias1, f_bup, f_bdown, f_gain2, f_bias2 = tuple(
        (item.astype(jnp.float32) for item in vectors)
    )
    proj = project_forward(layer_input, m_qkv) + f_bqkv
    pre_query = proj[:, :model_width].reshape(seqs_here, length, head_count, HD)
    pre_key = proj[:, model_width : 2 * model_width].reshape(seqs_here, length, head_count, HD)
    query = jax.nn.relu(pre_query) * 0.125
    keyed = jax.nn.relu(pre_key)
    q_feat = jnp.moveaxis(
        jnp.concatenate([query * cos_col, query * sin_col], axis=-1).astype(jnp.bfloat16), 2, 0
    )
    k_feat = jnp.moveaxis(
        jnp.concatenate([keyed * cos_col, keyed * sin_col], axis=-1).astype(jnp.bfloat16), 2, 0
    )
    v_bf = jnp.moveaxis(
        proj[:, 2 * model_width :].reshape(seqs_here, length, head_count, HD).astype(jnp.bfloat16),
        2,
        0,
    )

    def attend(pieces):
        q_part, k_part, v_part = pieces
        scores = (
            jnp.einsum("sid,sjd->sij", q_part, k_part, preferred_element_type=jnp.float32)
            * keep_mask
        )
        denom = jnp.maximum(jnp.sum(scores, axis=-1), 1.0)
        numer = jnp.einsum(
            "sij,sjd->sid", scores.astype(jnp.bfloat16), v_part, preferred_element_type=jnp.float32
        )
        return (numer, denom)

    numer, denom = lax.map(attend, (q_feat, k_feat, v_bf))
    attn_full = numer / denom[..., None]
    attn = jnp.moveaxis(attn_full, 0, 2).reshape(tokens, model_width).astype(jnp.bfloat16)
    branch = project_forward(attn, m_out) + f_bout
    resid_one = layer_input.astype(jnp.float32) + branch
    hidden, pull_one = jax.vjp(layer_norm, resid_one, f_gain1, f_bias1)
    hidden_bf = hidden.astype(jnp.bfloat16)
    upward = project_forward(hidden_bf, m_up) + f_bup
    action, pull_gelu = jax.vjp(gelu_exact, upward)
    action_bf = action.astype(jnp.bfloat16)
    downward = project_forward(action_bf, m_down) + f_bdown
    result, pull_two = jax.vjp(layer_norm, hidden + downward, f_gain2, f_bias2)
    d_resid_two, grad_gain2, grad_bias2 = pull_two(cotangent.astype(jnp.float32))
    d_down = d_resid_two.astype(jnp.bfloat16)
    grad_bdown = jnp.sum(d_down, axis=0, dtype=jnp.float32)
    grad_wdown = weight_grad(action_bf, d_down, m_down)
    d_action = project_back(d_down, m_down)
    (d_up_full,) = pull_gelu(d_action)
    d_up = d_up_full.astype(jnp.bfloat16)
    grad_bup = jnp.sum(d_up, axis=0, dtype=jnp.float32)
    grad_wup = weight_grad(hidden_bf, d_up, m_up)
    d_hidden = project_back(d_up, m_up) + d_resid_two
    d_resid_one, grad_gain1, grad_bias1 = pull_one(d_hidden)
    d_branch = d_resid_one.astype(jnp.bfloat16)
    grad_bout = jnp.sum(d_branch, axis=0, dtype=jnp.float32)
    grad_wout = weight_grad(attn, d_branch, m_out)
    d_attn = jnp.moveaxis(
        project_back(d_branch, m_out).reshape(seqs_here, length, head_count, HD), 2, 0
    )
    d_denom = jnp.where(denom > 1.0, -jnp.sum(d_attn * attn_full, axis=-1) / denom, 0.0)
    d_numer = (d_attn / denom[..., None]).astype(jnp.bfloat16)

    def attend_back(pieces):
        q_part, k_part, v_part, numer_grad, denom_grad = pieces
        scores = (
            jnp.einsum("sid,sjd->sij", q_part, k_part, preferred_element_type=jnp.float32)
            * keep_mask
        )
        score_grad = (
            jnp.einsum("sid,sjd->sij", numer_grad, v_part, preferred_element_type=jnp.float32)
            + denom_grad[..., None]
        )
        score_grad = jnp.where(keep_mask > 0.0, score_grad, 0.0).astype(jnp.bfloat16)
        q_grad = jnp.einsum("sij,sjd->sid", score_grad, k_part, preferred_element_type=jnp.float32)
        k_grad = jnp.einsum("sij,sid->sjd", score_grad, q_part, preferred_element_type=jnp.float32)
        v_grad = jnp.einsum(
            "sij,sid->sjd",
            scores.astype(jnp.bfloat16),
            numer_grad,
            preferred_element_type=jnp.float32,
        )
        return (q_grad, k_grad, v_grad)

    d_qfeat, d_kfeat, d_value = lax.map(attend_back, (q_feat, k_feat, v_bf, d_numer, d_denom))
    d_qfeat = jnp.moveaxis(d_qfeat, 0, 2)
    d_kfeat = jnp.moveaxis(d_kfeat, 0, 2)
    d_query = (d_qfeat[..., :HD] * cos_col + d_qfeat[..., HD:] * sin_col) * 0.125
    d_query = jnp.where(pre_query > 0.0, d_query, 0.0)
    d_keyed = d_kfeat[..., :HD] * cos_col + d_kfeat[..., HD:] * sin_col
    d_keyed = jnp.where(pre_key > 0.0, d_keyed, 0.0)
    d_valued = jnp.moveaxis(d_value, 0, 2)
    d_proj = jnp.concatenate(
        [
            d_query.reshape(tokens, model_width),
            d_keyed.reshape(tokens, model_width),
            d_valued.reshape(tokens, model_width),
        ],
        axis=1,
    ).astype(jnp.bfloat16)
    grad_bqkv = jnp.sum(d_proj, axis=0, dtype=jnp.float32)
    grad_wqkv = weight_grad(layer_input, d_proj, m_qkv)
    input_grad = (project_back(d_proj, m_qkv) + d_resid_one).astype(jnp.bfloat16)
    totals = reduce_grads(
        (
            grad_wqkv,
            grad_wout,
            grad_wup,
            grad_wdown,
            grad_bqkv,
            grad_bout,
            grad_gain1,
            grad_bias1,
            grad_bup,
            grad_bdown,
            grad_gain2,
            grad_bias2,
        )
    )
    return (
        result.astype(jnp.bfloat16),
        input_grad,
        totals[0],
        totals[4],
        totals[1],
        totals[5],
        totals[6],
        totals[7],
        totals[2],
        totals[8],
        totals[3],
        totals[9],
        totals[10],
        totals[11],
    )


def solution(mesh):
    return jax.shard_map(
        body,
        mesh=mesh,
        in_specs=(
            P(("dp", "mx", "my"), None),
            P("mx", "my"),
            P(("mx", "my")),
            P("mx", "my"),
            P(("mx", "my")),
            P(("mx", "my")),
            P(("mx", "my")),
            P("mx", "my"),
            P(("mx", "my")),
            P("mx", "my"),
            P(("mx", "my")),
            P(("mx", "my")),
            P(("mx", "my")),
            P(("dp", "mx", "my")),
            P(("dp", "mx", "my"), None),
            P(("dp", "mx", "my"), None),
        ),
        out_specs=(
            P(("dp", "mx", "my"), None),
            P(("dp", "mx", "my"), None),
            P("mx", "my"),
            P(("mx", "my")),
            P("mx", "my"),
            P(("mx", "my")),
            P(("mx", "my")),
            P(("mx", "my")),
            P("mx", "my"),
            P(("mx", "my")),
            P("mx", "my"),
            P(("mx", "my")),
            P(("mx", "my")),
            P(("mx", "my")),
        ),
        check_vma=False,
    )
```

profile of v0, /device:TPU:0, one launch (start us, length us, event | category | flops | bytes accessed | tf_op | source)
XLA Modules:
  0.0 724.5 jit_solution(8829298997838399889)
XLA Ops:
  14.9 13.2 %all-reduce.18 = (bf16[2304]{0:T(1024)(128)(2,1)S(1)}, bf16[768]{0:T(1024)(128)(2,1)S(1)}, bf16[768]{0:T(1024)(128)(2,1)S(1)}, bf16[768]{0:T(1024)(128)(2,1)S(1)...) all-reduce(bf16[2304]{0:T(1024)(128)(2,1)S(1)} %dynamic-update-slic, ...), channel_id=1, replica_groups=mesh['dp'=8,'mx'=2,'my'=2] {'mx','my'}, use_global_device_ids=true, to_apply=%add | all-reduce | flops 6144 | bytes 24576
  32.3 5.4 all-gather.4
  44.7 17.7 %all-gather.10.cloned.1.call-done = bf16[1536,1152]{1,0:T(8,128)(2,1)} async-done(((bf16[384,1152]{1,0:T(8,128)(2,1)}), bf16[1536,1152]{1,0:T(8,128)(2,1)}) %all-gather.10.cloned.1.call-update) | async-done | bytes 3538960 | tf_op jit(solution)/shard_map/all_gather | solution.py:75
  62.4 4.5 copy.202
  67.0 5.3 bitcast_add_fusion.1
  72.3 3.3 slice_maximum_fusion
  81.7 3.6 copy.204
  85.4 4.7 fusion.106
  103.1 52.9 %while.30 = (s32[]{:T(128)}, f32[12,1,1024,64]{2,3,1,0:T(8,128)}, f32[12,1,1024]{2,1,0:T(1,128)S(1)}, bf16[12,1,1024,128]{3,2,1,0:T(8,128)(2,1)}, bf16[12,1,1024...) while((s32[]{:T(128)}, f32[12,1,1024,64]{2,3,1,0:T(8,128)}, ...), condition=%wide.region_3.4_spmd.clone.clone, body=%wide.region_1.3_spmd.clone.sunk.clone | while | flops 415236096 | bytes 9476177 | solution.py:230
  156.6 4.8 slice_compare_fusion.1
  161.4 2.9 copy.217
  164.3 3.2 copy.231
  173.4 7.2 copy.215
  180.6 4.9 copy.219
  185.6 6.6 copy.213
  192.2 5.0 copy.221
  197.3 33.6 %multiply_convert_fusion = (bf16[1024,3072]{1,0:T(8,128)(2,1)S(1)}, f32[1024,3072]{1,0:T(8,128)}, f32[1024,3072,1]{1,0,2:T(8,128)}) fusion(f32[3072]{0:T(1024)S(1)} %bitcast.428, bf16[1024,2,384]{0,2,1:T(8,128)(2,1)S(1)} %bitcast.412, bf16[3072,384,2]{1,0,2:T(8,128)(2,1)S(1)} %bitcast.400), kind=kOutput, calls=%fused_computation.69 | convolution fusion | flops 5039456256 | bytes 37761024 | tf_op jit(solution)/shard_map/tid,ijdn->tjn/dot_general | solution.py:38
  231.0 5.3 fusion.127
  239.4 2.9 fusion.120
  242.3 16.7 %fusion.128 = (bf16[3072]{0:T(1024)(128)(2,1)S(1)}, bf16[1024,3072]{1,0:T(8,128)(2,1)}) fusion(f32[1024,3072]{1,0:T(8,128)} %get-tuple-element.376, bf16[1024,2,384]{0,2,1:T(8,128)(2,1)} %bitcast.414, bf16[3072,2,384]{2,0,1:T(8,128)(2,1)} %bitcast.396, f32[3072]{0:T(1024)S(1)} %bitcast.429, f32[1024,3072,1]{1,0,2:T(8,128)} %get-tuple-element.401), kind=kOutput, calls=%fused_computation.190 | convolution fusion | flops 4882166784 | bytes 37767168 | tf_op jit(solution)/shard_map/tjn,ijdn->tid/dot_general | solution.py:50
  259.0 11.3 %multiply_reduce_fusion = (bf16[768]{0:T(1024)(128)(2,1)S(1)}, f32[1024]{0:T(1024)S(1)}, bf16[768]{0:T(1024)(128)(2,1)S(1)}, f32[1024,768]{0,1:T(8,128)S(1)}) fusion(f32[1024,768]{0,1:T(8,128)S(1)} %copy-done.1, f32[1024]{0:T(1024)S(1)} %copy-done.33, f32[1024]{0:T(1024)S(1)} %copy-done.29, f32[768]{0:T(1024)S(1)} %copy-done.31, ...), kind=kOutput, calls=%fused_computation.135 | convolution fusion | flops 4845204480 | bytes 22057984 | tf_op jit(solution)/shard_map/tjn,ijdn->tid/dot_general | solution.py:50
  279.5 5.6 fusion.97
  285.2 117.9 %while.31 = (s32[]{:T(128)}, f32[12,1,1024,128]{2,3,0,1:T(8,128)}, f32[12,1,1024,128]{2,3,0,1:T(8,128)}, bf16[12,1,1024,64]{2,3,1,0:T(8,128)(2,1)}, bf16[12,1,10...) while((s32[]{:T(128)}, f32[12,1,1024,128]{2,3,0,1:T(8,128)}, ...), condition=%wide.region_14.15_spmd.clone.clone, body=%wide.region_13.14_spmd.clone.sunk.clone | while | flops 1088421888 | bytes 9208937 | solution.py:283
  302.0 2.8 fusion.196
  311.8 2.8 fusion.196
  321.7 2.8 fusion.196
  331.5 2.8 fusion.196
  341.3 2.8 fusion.196
  361.0 2.8 fusion.196
  370.8 2.8 fusion.196
  380.6 2.8 fusion.196
  390.4 2.8 fusion.196
  403.0 6.3 fusion.95
  412.5 5.2 fusion.84
  417.7 5.8 copy.237
  423.6 9.1 %convert_bitcast_fusion = bf16[2,2,1536,384]{2,3,0,1:T(8,128)(2,1)} fusion(bf16[1024,2,384,1]{0,2,3,1:T(8,128)(2,1)} %bitcast.415, bf16[128,2,8,1536]{3,2,1,0:T(8,128)(2,1)} %bitcast.432), kind=kOutput, calls=%fused_computation.99 | convolution fusion | flops 4834197504 | bytes 12582912 | tf_op jit(solution)/shard_map/tid,tjn->ijdn/dot_general | solution.py:62
  432.7 6.9 copy.244
  439.6 15.3 %reshape.597 = bf16[1024,2,1536]{2,1,0:T(2,128)(2,1)} reshape(bf16[1024,3072]{1,0:T(8,128)(2,1)} %get-tuple-element.406) | data formatting | bytes 12582912 | tf_op jit(solution)/shard_map/reshape | solution.py:52
  454.9 10.6 %convert_bitcast_fusion.1 = bf16[2,2,384,1536]{2,3,0,1:T(8,128)(2,1)} fusion(bf16[1024,2,384,1]{0,2,1,3:T(8,128)(2,1)} %bitcast.413, bf16[1024,2,1536,1]{2,1,0,3:T(2,128)(2,1)} %bitcast.386), kind=kOutput, calls=%fused_computation.100 | convolution fusion | flops 4834197504 | bytes 12582912 | tf_op jit(solution)/shard_map/tid,tjn->ijdn/dot_general | solution.py:62
  465.5 6.7 copy.242
  472.3 42.8 %reduce-scatter.11.cloned.1.call-done = bf16[1,1536,384]{2,1,0:T(8,128)(2,1)} async-done(((bf16[4,1536,384]{2,1,0:T(8,128)(2,1)}), bf16[1,1536,384]{2,1,0:T(8,128)(2,1)}) %reduce-scatter.11.cloned.1.call-update) | async-done | bytes 1179664 | tf_op jit(solution)/shard_map/reduce_scatter | solution.py:110
  515.0 50.6 %reduce-scatter.9.cloned.1.call-done = bf16[1,384,1536]{2,1,0:T(8,128)(2,1)} async-done(((bf16[4,384,1536]{2,1,0:T(8,128)(2,1)}), bf16[1,384,1536]{2,1,0:T(8,128)(2,1)}) %reduce-scatter.9.cloned.1.call-update) | async-done | bytes 1179664 | tf_op jit(solution)/shard_map/reduce_scatter | solution.py:107
  569.5 4.0 copy.233
  573.6 10.7 %all-reduce.17 = (bf16[768]{0:T(1024)(128)(2,1)S(1)}, bf16[2304]{0:T(1024)(128)(2,1)S(1)}, bf16[768]{0:T(1024)(128)(2,1)S(1)}, bf16[768]{0:T(1024)(128)(2,1)S(1)...) all-reduce(bf16[768]{0:T(1024)(128)(2,1)S(1)} %dynamic-update-slice, ...), channel_id=1, replica_groups=mesh['dp'=8,'mx'=2,'my'=2] {'mx','my'}, use_global_device_ids=true, to_apply=%add.6 | all-reduce | flops 10752 | bytes 43008
  584.9 23.7 %all-reduce.15 = (bf16[576]{0:T(1024)(128)(2,1)S(1)}, bf16[192]{0:T(256)(128)(2,1)S(1)}, bf16[192]{0:T(256)(128)(2,1)S(1)}, bf16[192]{0:T(256)(128)(2,1)S(1)}, b...) all-reduce(bf16[576]{0:T(1024)(128)(2,1)S(1)} %dynamic-slice.8, ...), channel_id=1, replica_groups=mesh['dp'=8,'mx'=2,'my'=2] {'dp'}, use_global_device_ids=true, to_apply=%region_19.20 | all-reduce | flops 2496 | bytes 9984 | tf_op jit(solution)/shard_map/psum | solution.py:144
  613.1 9.3 %fusion.98 = bf16[1024,768]{0,1:T(8,128)(2,1)} fusion(f32[1024,768]{0,1:T(8,128)} %copy-done.4, bf16[768,2,1152]{2,0,1:T(8,128)(2,1)} %bitcast.404, bf16[1024,2,1152]{0,2,1:T(8,128)(2,1)} %bitcast.394, f32[1024]{0:T(1024)S(1)} %negate_multiply_fusion.1), kind=kOutput, calls=%fused_computation.128 | convolution fusion | flops 3626237952 | bytes 12980224 | tf_op jit(solution)/shard_map/tjn,ijdn->tid/dot_general | solution.py:50
  629.3 81.4 %all-reduce.21.cloned.1.call-done = (bf16[384,1152]{1,0:T(8,128)(2,1)}, bf16[384,384]{1,0:T(8,128)(2,1)}, bf16[384,1536]{1,0:T(8,128)(2,1)}, bf16[1536,384]{1,0:T(8,128)(2,1)}) async-done(((bf16[384,1152]{1,0:T(8,128)(2,1)}, bf16[384,384]{1,0:T(8,128)(2,1)}, bf16[384,1536]{1,0:T(8,128)(2,1)}, bf16[1536,384]{1,0:T(8,128)(2,1)}), (bf16[384,1152]{1,0:T(8,128)(2,1)}, bf16[384,384]{1,0:T(8,128)(2,1)}, ...) | async-done | bytes 3538960 | tf_op jit(solution)/shard_map/psum | solution.py:140
  710.7 3.1 convert_element_type.319
  (338 shorter events, 221.3 us)
Async XLA Ops:
  7.2 6.2 copy-start.55
  7.2 6.5 copy-start.56
  7.2 6.7 copy-start.57
  7.2 6.9 copy-start.58
  7.2 7.2 copy-start.59
  7.2 7.4 %copy-start.52 = (bf16[576]{0:T(1024)(128)(2,1)S(1)}, bf16[576]{0:T(1024)(128)(2,1)}, u32[]{:S(2)}) copy-start(bf16[576]{0:T(1024)(128)(2,1)} %param.22) | copy-start | bytes 3460
  7.3 21.4 %copy-start.54 = (s32[1,8]{1,0:T(1,128)S(1)}, s32[1,8]{1,0:T(1,128)}, u32[]{:S(2)}) copy-start(s32[1,8]{1,0:T(1,128)} %param.34) | copy-start | bytes 100
  7.3 21.4 %copy-start.48 = (s32[1024]{0:T(1024)S(1)}, s32[1024]{0:T(1024)}, u32[]{:S(2)}) copy-start(s32[1024]{0:T(1024)} %param.33) | copy-start | bytes 12292
  7.3 22.7 %copy-start.12 = (bf16[1024,768]{1,0:T(8,128)(2,1)S(1)}, bf16[1024,768]{1,0:T(8,128)(2,1)}, u32[]{:S(2)}) copy-start(bf16[1024,768]{1,0:T(8,128)(2,1)} %param.20) | copy-start | bytes 4718596
  7.3 33.8 %all-gather.12.cloned.1.call-start = ((), (), s32[]{:S(2)}) async-start(), calls=%async_computation.9 | async-start | bytes 1474560 | tf_op jit(solution)/shard_map/all_gather | solution.py:76
  8.0 54.4 %all-gather.10.cloned.1.call-start = ((), (), s32[]{:S(2)}) async-start(), calls=%async_computation.8 | async-start | bytes 4423680 | tf_op jit(solution)/shard_map/all_gather | solution.py:75
  8.8 164.6 %all-gather.16.cloned.1.call-start = ((), (), s32[]{:S(2)}) async-start(), calls=%async_computation.11 | async-start | bytes 5898240 | tf_op jit(solution)/shard_map/all_gather | solution.py:78
  9.5 22.7 %copy-start.53 = (bf16[768]{0:T(1024)(128)(2,1)S(1)}, bf16[768]{0:T(1024)(128)(2,1)}, u32[]{:S(2)}) copy-start(bf16[768]{0:T(1024)(128)(2,1)} %param.28) | copy-start | bytes 4612
  9.5 29.9 %copy-start.5 = (bf16[1024,768]{1,0:T(8,128)(2,1)S(1)}, bf16[1024,768]{1,0:T(8,128)(2,1)}, u32[]{:S(2)}) copy-start(bf16[1024,768]{1,0:T(8,128)(2,1)} %param.35) | copy-start | bytes 4718596
  9.5 176.1 %all-gather.14.cloned.1.call-start = ((), (), s32[]{:S(2)}) async-start(), calls=%async_computation.10 | async-start | bytes 5898240 | tf_op jit(solution)/shard_map/all_gather | solution.py:77
  10.1 462.1 %reduce-scatter.7.cloned.1.call-start = ((), (), s32[]{:S(2)}) async-start(), calls=%async_computation.5 | async-start | bytes 1474560 | tf_op jit(solution)/shard_map/reduce_scatter | solution.py:104
  29.4 55.9 %copy-start.36 = (f32[1024]{0:T(1024)}, f32[1024]{0:T(1024)S(1)}, u32[]{:S(2)}) copy-start(f32[1024]{0:T(1024)S(1)} %get-tuple-element.393) | copy-start | bytes 12292
  29.4 55.9 %copy-start.38 = (f32[1024]{0:T(1024)}, f32[1024]{0:T(1024)S(1)}, u32[]{:S(2)}) copy-start(f32[1024]{0:T(1024)S(1)} %get-tuple-element.396) | copy-start | bytes 12292
  31.6 140.0 %copy-start.30 = (f32[768]{0:T(1024)}, f32[768]{0:T(1024)S(1)}, u32[]{:S(2)}) copy-start(f32[768]{0:T(1024)S(1)} %convert_element_type.283) | copy-start | bytes 9220
  72.3 5.8 copy-start.3
  156.6 10.9 %copy-start.22 = (f32[12,1,1024]{2,0,1:T(8,128)}, f32[12,1,1024]{2,0,1:T(8,128)S(1)}, u32[]{:S(2)}) copy-start(f32[12,1,1024]{2,0,1:T(8,128)S(1)} %copy.322) | copy-start | bytes 147460
  161.4 6.1 copy-start.10
  171.7 9.0 %copy-start.34 = (f32[1024]{0:T(1024)}, f32[1024]{0:T(1024)S(1)}, u32[]{:S(2)}) copy-start(f32[1024]{0:T(1024)S(1)} %multiply_reduce_fusion.3) | copy-start | bytes 12292
  172.9 7.8 %copy-start.32 = (f32[1024]{0:T(1024)}, f32[1024]{0:T(1024)S(1)}, u32[]{:S(2)}) copy-start(f32[1024]{0:T(1024)S(1)} %fusion.115) | copy-start | bytes 12292
  173.4 23.8 %copy-start.15 = (bf16[1024,768]{0,1:T(8,128)(2,1)}, bf16[1024,768]{0,1:T(8,128)(2,1)S(1)}, u32[]{:S(2)}) copy-start(bf16[1024,768]{0,1:T(8,128)(2,1)S(1)} %fusion.101) | copy-start | bytes 4718596
  192.2 5.0 copy-start.43
  192.2 38.7 %slice-start = ((s8[4718592]{0:T(1024)(128)(4,1)}), s8[524288]{0:T(1024)(128)(4,1)S(1)}, s32[]{:S(2)}) async-start(s8[4718592]{0:T(1024)(128)(4,1)} %bitcast.397), calls=%async_computation.13 | async-start | bytes 1048576
  197.2 33.7 %copy-start.1 = (f32[1024,768]{0,1:T(8,128)S(1)}, f32[1024,768]{0,1:T(8,128)}, u32[]{:S(2)}) copy-start(f32[1024,768]{0,1:T(8,128)} %copy-done) | copy-start | bytes 9437188
  197.2 33.7 %slice-start.1 = ((s8[4718592]{0:T(1024)(128)(4,1)}), s8[4194304]{0:T(1024)(128)(4,1)S(1)}, s32[]{:S(2)}) async-start(s8[4718592]{0:T(1024)(128)(4,1)} %bitcast.397), calls=%async_computation.14 | async-start | bytes 8388608
  197.3 33.7 %copy-start.29 = (f32[1024]{0:T(1024)S(1)}, f32[1024]{0:T(1024)}, u32[]{:S(2)}) copy-start(f32[1024]{0:T(1024)} %copy-done.28) | copy-start | bytes 12292
  197.3 33.7 %copy-start.31 = (f32[768]{0:T(1024)S(1)}, f32[768]{0:T(1024)}, u32[]{:S(2)}) copy-start(f32[768]{0:T(1024)} %copy-done.30) | copy-start | bytes 9220
  197.3 33.7 %copy-start.33 = (f32[1024]{0:T(1024)S(1)}, f32[1024]{0:T(1024)}, u32[]{:S(2)}) copy-start(f32[1024]{0:T(1024)} %copy-done.32) | copy-start | bytes 12292
  197.3 33.7 %copy-start.42 = (f32[768]{0:T(1024)S(1)}, f32[768]{0:T(1024)}, u32[]{:S(2)}) copy-start(f32[768]{0:T(1024)} %convert_element_type.284) | copy-start | bytes 9220
  197.3 33.7 %copy-start.46 = (f32[768]{0:T(1024)S(1)}, f32[768]{0:T(1024)}, u32[]{:S(2)}) copy-start(f32[768]{0:T(1024)} %convert_element_type.288) | copy-start | bytes 9220
  230.9 5.4 copy-start.61
  231.0 5.3 copy-start.2
  231.0 5.3 copy-start.27
  259.0 11.3 %copy-start.35 = (f32[1024]{0:T(1024)S(1)}, f32[1024]{0:T(1024)}, u32[]{:S(2)}) copy-start(f32[1024]{0:T(1024)} %copy-done.34) | copy-start | bytes 12292
  279.4 192.9 %reduce-scatter.5.cloned.1.call-start = ((), (), s32[]{:S(2)}) async-start(), calls=%async_computation.4 | async-start | bytes 4423680 | tf_op jit(solution)/shard_map/reduce_scatter | solution.py:101
  279.5 5.6 copy-start.26
  279.5 5.7 copy-start.50
  285.2 117.9 %copy-start.37 = (f32[1024]{0:T(1024)S(1)}, f32[1024]{0:T(1024)}, u32[]{:S(2)}) copy-start(f32[1024]{0:T(1024)} %copy-done.36) | copy-start | bytes 12292
  285.2 117.9 %copy-start.39 = (f32[1024]{0:T(1024)S(1)}, f32[1024]{0:T(1024)}, u32[]{:S(2)}) copy-start(f32[1024]{0:T(1024)} %copy-done.38) | copy-start | bytes 12292
  403.0 6.3 copy-start.6
  423.6 91.5 %reduce-scatter.11.cloned.1.call-start = ((), (), s32[]{:S(2)}) async-start(), calls=%async_computation.7 | async-start | bytes 5898240 | tf_op jit(solution)/shard_map/reduce_scatter | solution.py:110
  439.6 126.0 %reduce-scatter.9.cloned.1.call-start = ((), (), s32[]{:S(2)}) async-start(), calls=%async_computation.6 | async-start | bytes 5898240 | tf_op jit(solution)/shard_map/reduce_scatter | solution.py:107
  472.2 97.1 %copy-start.60 = (bf16[192]{0:T(256)(128)(2,1)S(1)}, bf16[192]{0:T(256)(128)(2,1)}, u32[]{:S(2)}) copy-start(bf16[192]{0:T(256)(128)(2,1)} %param.32) | copy-start | bytes 1156
  472.2 238.5 %all-reduce.21.cloned.1.call-start = ((), (), s32[]{:S(2)}) async-start(), calls=%async_computation.12 | async-start | bytes 7077888 | tf_op jit(solution)/shard_map/psum | solution.py:140
  (25 other events, 70.1 us)
Sparse Core Ops, SparseCore 0:
  9.7 20.3 all-gather.11
  31.6 30.7 all-gather.9
  64.0 37.4 all-gather.15
  102.9 37.4 all-gather.13
  279.5 26.1 reduce-scatter.6
  423.7 40.8 reduce-scatter.4
  467.2 47.8 reduce-scatter.10
  517.7 47.8 reduce-scatter.8
  569.6 141.0 all-reduce.20
where the time goes:
time: 731 us; the launch traced here: 725 us
  matrix products  286 us (39%)
  waiting for transfers between devices  195 us (27%)
  local copies, waits for them, and re-layouts  119 us (16%)
  blocking collectives  52.9 us (7%)
  other arithmetic  51.9 us (7%)
  between operations  18.4 us (3%)
    psum x1, waiting for transfers between devices, reduce_grads(): lax.psum(blocks[0].astype(jnp.bfloat16), 'dp').astype(jnp.float32)  81.4 us
    reduce_scatter x1, waiting for transfers between devices, reduce_grads(): lax.psum_scatter(grads[2].astype(jnp.bfloat16), ('mx', 'my'), scatter_dim...  50.6 us
    dot_general x4, matrix products, project_forward(): jnp.einsum('tid,ijdn->tjn', operand.reshape(rows_here, grid_rows, row_siz...  45.6 us
    dot_general x4, matrix products, project_back(): jnp.einsum('tjn,ijdn->tid', grad_rows.reshape(rows_here, grid_cols, col_s...  42.9 us
    reduce_scatter x1, waiting for transfers between devices, reduce_grads(): lax.psum_scatter(grads[3].astype(jnp.bfloat16), ('mx', 'my'), scatter_dim...  42.8 us
    dot_general x12, matrix products, attend_back(): jnp.einsum('sij,sid->sjd', scores.astype(jnp.bfloat16), numer_grad, prefe...  33.9 us
    reshape x6, local copies, waits for them, and re-layouts, fetch_weights(): piece.reshape(grid_rows, grid_cols, piece.shape[1], piece.shape[2])  32.3 us
    dot_general x12, matrix products, attend_back(): jnp.einsum('sij,sjd->sid', score_grad, k_part, preferred_element_type=jnp...  31.1 us
  transfers between devices with their start and end apart: 9, of which 4 were waited for; matrix products, arithmetic and copies ran while one was open for 48% of the time, Pallas kernels for 0%

commit v1 on v0

--- a/solution.py
+++ b/solution.py
@@ -137,7 +137,7 @@
     )
     blocks = tuple((piece[0] for piece in summed[:4])) + tuple(summed[4:])
     return (
-        lax.psum(blocks[0].astype(jnp.bfloat16), "dp").astype(jnp.float32),
+        jnp.sum(lax.all_gather(blocks[0].astype(jnp.bfloat16), "dp"), axis=0).astype(jnp.float32),
         lax.psum(blocks[1].astype(jnp.bfloat16), "dp").astype(jnp.float32),
         lax.psum(blocks[2].astype(jnp.bfloat16), "dp").astype(jnp.float32),
         lax.psum(blocks[3].astype(jnp.bfloat16), "dp").astype(jnp.float32),

time: 731 us -> 768 us (1.051)
  waiting for transfers between devices: 195 us -> 226 us
    all_gather x0 -> x1, waiting for transfers between devices: none -> 104 us  [reduce_grads(): lax.all_gather(blocks[0].astype(jnp.bfloat16), 'dp')]
    reduce_scatter x1, waiting for transfers between devices: 50.6 us -> 0.02 us  [reduce_grads(): lax.psum_scatter(grads[2].astype(jnp.bfloat16), ('mx', 'my'), scatter_dim...]
    reduce_scatter x1, waiting for transfers between devices: 42.8 us -> 0.02 us  [reduce_grads(): lax.psum_scatter(grads[3].astype(jnp.bfloat16), ('mx', 'my'), scatter_dim...]
    reduce_scatter x1, waiting for transfers between devices: 0.02 us -> 40.2 us  [reduce_grads(): lax.psum_scatter(grads[0].astype(jnp.bfloat16), ('mx', 'my'), scatter_dim...]
    psum x1, waiting for transfers between devices: 81.4 us -> 58.1 us  [reduce_grads(): lax.psum(blocks[1].astype(jnp.bfloat16), 'dp').astype(jnp.float32)]
    unnamed x160 -> x154, local copies, waits for them, and re-layouts: 31.1 us -> 29.4 us
  transfers between devices with their start and end apart: 9 -> 10, of which waited for: 4 -> 4; matrix products, arithmetic and copies ran while one was open for 48% -> 47% of each run, Pallas kernels for 0% -> 0%
where the time goes in v1:
time: 768 us; the launch traced here: 761 us
  matrix products  287 us (37%)
  waiting for transfers between devices  226 us (29%)
  local copies, waits for them, and re-layouts  118 us (15%)
  other arithmetic  58.3 us (8%)
  blocking collectives  52.6 us (7%)
  between operations  18.5 us (2%)
    all_gather x1, waiting for transfers between devices, reduce_grads(): lax.all_gather(blocks[0].astype(jnp.bfloat16), 'dp')  104 us
    psum x1, waiting for transfers between devices, reduce_grads(): lax.psum(blocks[1].astype(jnp.bfloat16), 'dp').astype(jnp.float32)  58.1 us
    dot_general x4, matrix products, project_forward(): jnp.einsum('tid,ijdn->tjn', operand.reshape(rows_here, grid_rows, row_siz...  45.5 us
    dot_general x4, matrix products, project_back(): jnp.einsum('tjn,ijdn->tid', grad_rows.reshape(rows_here, grid_cols, col_s...  43 us
    reduce_scatter x1, waiting for transfers between devices, reduce_grads(): lax.psum_scatter(grads[0].astype(jnp.bfloat16), ('mx', 'my'), scatter_dim...  40.2 us
    dot_general x12, matrix products, attend_back(): jnp.einsum('sij,sid->sjd', scores.astype(jnp.bfloat16), numer_grad, prefe...  34 us
    reshape x6, local copies, waits for them, and re-layouts, fetch_weights(): piece.reshape(grid_rows, grid_cols, piece.shape[1], piece.shape[2])  32.3 us
    dot_general x12, matrix products, attend_back(): jnp.einsum('sij,sjd->sid', score_grad, k_part, preferred_element_type=jnp...  31.1 us
  transfers between devices with their start and end apart: 10, of which 4 were waited for; matrix products, arithmetic and copies ran while one was open for 47% of the time, Pallas kernels for 0%

profile of v1, /device:TPU:0, one launch (start us, length us, event | category | flops | bytes accessed | tf_op | source)
XLA Modules:
  0.0 761.2 jit_solution(16829244715967930198)
XLA Ops:
  13.5 13.2 %all-reduce.18 = (bf16[2304]{0:T(1024)(128)(2,1)S(1)}, bf16[768]{0:T(1024)(128)(2,1)S(1)}, bf16[768]{0:T(1024)(128)(2,1)S(1)}, bf16[768]{0:T(1024)(128)(2,1)S(1)...) all-reduce(bf16[2304]{0:T(1024)(128)(2,1)S(1)} %dynamic-update-slic, ...), channel_id=1, replica_groups=mesh['dp'=8,'mx'=2,'my'=2] {'mx','my'}, use_global_device_ids=true, to_apply=%add | all-reduce | flops 6144 | bytes 24576
  30.9 5.2 all-gather.4
  42.3 20.1 %all-gather.13.cloned.1.call-done = bf16[1536,1152]{1,0:T(8,128)(2,1)} async-done(((bf16[384,1152]{1,0:T(8,128)(2,1)}), bf16[1536,1152]{1,0:T(8,128)(2,1)}) %all-gather.13.cloned.1.call-update) | async-done | bytes 3538960 | tf_op jit(solution)/shard_map/all_gather | solution.py:75
  62.4 4.5 copy.202
  66.9 5.3 bitcast_add_fusion.1
  72.2 3.3 slice_maximum_fusion
  81.6 3.5 copy.204
  85.2 4.7 fusion.106
  90.3 2.8 copy.208
  102.9 53.0 %while.30 = (s32[]{:T(128)}, f32[12,1,1024,64]{2,3,1,0:T(8,128)}, f32[12,1,1024]{2,1,0:T(1,128)S(1)}, bf16[12,1,1024,128]{3,2,1,0:T(8,128)(2,1)}, bf16[12,1,1024...) while((s32[]{:T(128)}, f32[12,1,1024,64]{2,3,1,0:T(8,128)}, ...), condition=%wide.region_3.4_spmd.clone.clone, body=%wide.region_1.3_spmd.clone.sunk.clone | while | flops 415236096 | bytes 9476177 | solution.py:230
  162.3 7.3 copy.215
  169.5 4.9 copy.219
  174.5 6.6 copy.213
  181.1 4.9 copy.221
  186.1 33.6 %multiply_convert_fusion = (bf16[1024,3072]{1,0:T(8,128)(2,1)S(1)}, f32[1024,3072]{1,0:T(8,128)}, f32[1024,3072,1]{1,0,2:T(8,128)}) fusion(f32[3072]{0:T(1024)S(1)} %bitcast.426, bf16[1024,2,384]{0,2,1:T(8,128)(2,1)S(1)} %bitcast.411, bf16[3072,384,2]{1,0,2:T(8,128)(2,1)S(1)} %bitcast.399), kind=kOutput, calls=%fused_computation.69 | convolution fusion | flops 5039456256 | bytes 37761024 | tf_op jit(solution)/shard_map/tid,ijdn->tjn/dot_general | solution.py:38
  219.8 5.3 fusion.127
  228.1 2.9 fusion.120
  231.0 16.8 %fusion.128 = (bf16[3072]{0:T(1024)(128)(2,1)S(1)}, bf16[1024,3072]{1,0:T(8,128)(2,1)}) fusion(f32[1024,3072]{1,0:T(8,128)} %get-tuple-element.375, bf16[1024,2,384]{0,2,1:T(8,128)(2,1)} %bitcast.415, bf16[3072,2,384]{2,0,1:T(8,128)(2,1)} %bitcast.395, f32[3072]{0:T(1024)S(1)} %bitcast.427, f32[1024,3072,1]{1,0,2:T(8,128)} %get-tuple-element.400), kind=kOutput, calls=%fused_computation.190 | convolution fusion | flops 4882166784 | bytes 37767168 | tf_op jit(solution)/shard_map/tjn,ijdn->tid/dot_general | solution.py:50
  247.8 11.2 %multiply_reduce_fusion = (bf16[768]{0:T(1024)(128)(2,1)S(1)}, f32[1024]{0:T(1024)S(1)}, bf16[768]{0:T(1024)(128)(2,1)S(1)}, f32[1024,768]{0,1:T(8,128)S(1)}) fusion(f32[1024,768]{0,1:T(8,128)S(1)} %copy-done.1, f32[1024]{0:T(1024)S(1)} %copy-done.30, f32[1024]{0:T(1024)S(1)} %copy-done.26, f32[768]{0:T(1024)S(1)} %copy-done.28, ...), kind=kOutput, calls=%fused_computation.135 | convolution fusion | flops 4845204480 | bytes 22057984 | tf_op jit(solution)/shard_map/tjn,ijdn->tid/dot_general | solution.py:50
  268.2 9.1 %convert_bitcast_fusion = bf16[2,2,1536,384]{2,3,0,1:T(8,128)(2,1)} fusion(bf16[1024,2,384,1]{0,2,3,1:T(8,128)(2,1)} %bitcast.416, bf16[128,2,8,1536]{3,2,1,0:T(8,128)(2,1)} %bitcast.430), kind=kOutput, calls=%fused_computation.99 | convolution fusion | flops 4834197504 | bytes 12582912 | tf_op jit(solution)/shard_map/tid,tjn->ijdn/dot_general | solution.py:62
  277.3 6.7 copy.244
  287.8 4.8 slice_compare_fusion.1
  298.1 15.1 %reshape.596 = bf16[1024,2,1536]{2,1,0:T(2,128)(2,1)} reshape(bf16[1024,3072]{1,0:T(8,128)(2,1)} %get-tuple-element.405) | data formatting | bytes 12582912 | tf_op jit(solution)/shard_map/reshape | solution.py:52
  313.3 10.6 %convert_bitcast_fusion.1 = bf16[2,2,384,1536]{2,3,0,1:T(8,128)(2,1)} fusion(bf16[1024,2,384,1]{0,2,1,3:T(8,128)(2,1)} %bitcast.412, bf16[1024,2,1536,1]{2,1,0,3:T(2,128)(2,1)} %bitcast.385), kind=kOutput, calls=%fused_computation.100 | convolution fusion | flops 4834197504 | bytes 12582912 | tf_op jit(solution)/shard_map/tid,tjn->ijdn/dot_general | solution.py:62
  323.9 6.7 copy.242
  330.6 5.7 fusion.97
  336.9 118.5 %while.31 = (s32[]{:T(128)}, f32[12,1,1024,128]{2,3,0,1:T(8,128)}, f32[12,1,1024,128]{2,3,0,1:T(8,128)}, bf16[12,1,1024,64]{2,3,1,0:T(8,128)(2,1)}, bf16[12,1,10...) while((s32[]{:T(128)}, f32[12,1,1024,128]{2,3,0,1:T(8,128)}, ...), condition=%wide.region_14.15_spmd.clone.clone, body=%wide.region_13.14_spmd.clone.sunk.clone | while | flops 1088421888 | bytes 9208937 | solution.py:283
  344.3 2.9 fusion.196
  354.2 2.9 fusion.196
  364.1 2.8 fusion.196
  374.0 2.8 fusion.196
  383.9 2.8 fusion.196
  403.4 2.8 fusion.196
  413.3 2.8 fusion.196
  423.1 2.8 fusion.196
  452.6 2.8 fusion.196
  455.4 6.3 fusion.95
  464.8 5.3 fusion.84
  470.0 5.8 copy.237
  476.6 40.2 %reduce-scatter.5.cloned.1.call-done = bf16[1,384,1152]{2,1,0:T(8,128)(2,1)} async-done(((bf16[4,384,1152]{2,1,0:T(8,128)(2,1)}), bf16[1,384,1152]{2,1,0:T(8,128)(2,1)}) %reduce-scatter.5.cloned.1.call-update) | async-done | bytes 884752 | tf_op jit(solution)/shard_map/reduce_scatter | solution.py:101
  520.8 4.1 copy.233
  524.9 10.7 %all-reduce.17 = (bf16[768]{0:T(1024)(128)(2,1)S(1)}, bf16[2304]{0:T(1024)(128)(2,1)S(1)}, bf16[768]{0:T(1024)(128)(2,1)S(1)}, bf16[768]{0:T(1024)(128)(2,1)S(1)...) all-reduce(bf16[768]{0:T(1024)(128)(2,1)S(1)} %dynamic-update-slice, ...), channel_id=1, replica_groups=mesh['dp'=8,'mx'=2,'my'=2] {'mx','my'}, use_global_device_ids=true, to_apply=%add.6 | all-reduce | flops 10752 | bytes 43008
  536.2 23.6 %all-reduce.15 = (bf16[576]{0:T(1024)(128)(2,1)S(1)}, bf16[192]{0:T(256)(128)(2,1)S(1)}, bf16[192]{0:T(256)(128)(2,1)S(1)}, bf16[192]{0:T(256)(128)(2,1)S(1)}, b...) all-reduce(bf16[576]{0:T(1024)(128)(2,1)S(1)} %dynamic-slice.8, ...), channel_id=1, replica_groups=mesh['dp'=8,'mx'=2,'my'=2] {'dp'}, use_global_device_ids=true, to_apply=%region_19.20 | all-reduce | flops 2496 | bytes 9984 | tf_op jit(solution)/shard_map/psum | solution.py:144
  564.3 9.3 %fusion.98 = bf16[1024,768]{0,1:T(8,128)(2,1)} fusion(f32[1024,768]{0,1:T(8,128)} %copy-done.4, bf16[768,2,1152]{2,0,1:T(8,128)(2,1)} %bitcast.403, bf16[1024,2,1152]{0,2,1:T(8,128)(2,1)} %bitcast.393, f32[1024]{0:T(1024)S(1)} %negate_multiply_fusion.1), kind=kOutput, calls=%fused_computation.128 | convolution fusion | flops 3626237952 | bytes 12980224 | tf_op jit(solution)/shard_map/tjn,ijdn->tid/dot_general | solution.py:50
  580.4 58.1 %all-reduce.21.cloned.1.call-done = (bf16[384,384]{1,0:T(8,128)(2,1)}, bf16[384,1536]{1,0:T(8,128)(2,1)}, bf16[1536,384]{1,0:T(8,128)(2,1)}) async-done(((bf16[384,384]{1,0:T(8,128)(2,1)}, bf16[384,1536]{1,0:T(8,128)(2,1)}, bf16[1536,384]{1,0:T(8,128)(2,1)}), (bf16[384,384]{1,0:T(8,128)(2,1)}, bf16[384,1536]{1,0:T(8,128)(2,1)}, bf16[1536,384]{1,0:T(8,128)(2,1)})) %all-reduce.21.cloned.1.call-update) | async-done | bytes 2654224 | tf_op jit(solution)/shard_map/psum | solution.py:141
  638.5 3.1 convert_element_type.318
  644.0 104.4 %all-gather.11.cloned.1.call-done = bf16[8,384,1152]{2,1,0:T(8,128)(2,1)} async-done(((bf16[1,384,1152]{2,1,0:T(8,128)(2,1)}), bf16[8,384,1152]{2,1,0:T(8,128)(2,1)}) %all-gather.11.cloned.1.call-update) | async-done | bytes 7077904 | tf_op jit(solution)/shard_map/all_gather | solution.py:140
  748.4 4.5 reduce_sum.240
  (336 shorter events, 226.5 us)
Async XLA Ops:
  7.2 4.9 copy-start.52
  7.2 5.2 copy-start.53
  7.2 5.4 copy-start.54
  7.2 5.6 copy-start.55
  7.2 5.8 copy-start.56
  7.2 6.1 copy-start.49
  7.3 20.1 %copy-start.51 = (s32[1,8]{1,0:T(1,128)S(1)}, s32[1,8]{1,0:T(1,128)}, u32[]{:S(2)}) copy-start(s32[1,8]{1,0:T(1,128)} %param.34) | copy-start | bytes 100
  7.3 20.1 %copy-start.45 = (s32[1024]{0:T(1024)S(1)}, s32[1024]{0:T(1024)}, u32[]{:S(2)}) copy-start(s32[1024]{0:T(1024)} %param.33) | copy-start | bytes 12292
  7.3 21.4 %copy-start.10 = (bf16[1024,768]{1,0:T(8,128)(2,1)S(1)}, bf16[1024,768]{1,0:T(8,128)(2,1)}, u32[]{:S(2)}) copy-start(bf16[1024,768]{1,0:T(8,128)(2,1)} %param.20) | copy-start | bytes 4718596
  7.3 32.5 %all-gather.15.cloned.1.call-start = ((), (), s32[]{:S(2)}) async-start(), calls=%async_computation.10 | async-start | bytes 1474560 | tf_op jit(solution)/shard_map/all_gather | solution.py:76
  8.0 22.9 %copy-start.50 = (bf16[768]{0:T(1024)(128)(2,1)S(1)}, bf16[768]{0:T(1024)(128)(2,1)}, u32[]{:S(2)}) copy-start(bf16[768]{0:T(1024)(128)(2,1)} %param.28) | copy-start | bytes 4612
  8.0 29.8 %copy-start.5 = (bf16[1024,768]{1,0:T(8,128)(2,1)S(1)}, bf16[1024,768]{1,0:T(8,128)(2,1)}, u32[]{:S(2)}) copy-start(bf16[1024,768]{1,0:T(8,128)(2,1)} %param.35) | copy-start | bytes 4718596
  8.0 54.4 %all-gather.13.cloned.1.call-start = ((), (), s32[]{:S(2)}) async-start(), calls=%async_computation.9 | async-start | bytes 4423680 | tf_op jit(solution)/shard_map/all_gather | solution.py:75
  8.8 153.5 %all-gather.19.cloned.1.call-start = ((), (), s32[]{:S(2)}) async-start(), calls=%async_computation.12 | async-start | bytes 5898240 | tf_op jit(solution)/shard_map/all_gather | solution.py:78
  9.5 164.9 %all-gather.17.cloned.1.call-start = ((), (), s32[]{:S(2)}) async-start(), calls=%async_computation.11 | async-start | bytes 5898240 | tf_op jit(solution)/shard_map/all_gather | solution.py:77
  10.1 465.8 %reduce-scatter.7.cloned.1.call-start = ((), (), s32[]{:S(2)}) async-start(), calls=%async_computation.6 | async-start | bytes 1474560 | tf_op jit(solution)/shard_map/reduce_scatter | solution.py:104
  28.1 57.1 %copy-start.33 = (f32[1024]{0:T(1024)}, f32[1024]{0:T(1024)S(1)}, u32[]{:S(2)}) copy-start(f32[1024]{0:T(1024)S(1)} %get-tuple-element.392) | copy-start | bytes 12292
  28.1 57.1 %copy-start.35 = (f32[1024]{0:T(1024)}, f32[1024]{0:T(1024)S(1)}, u32[]{:S(2)}) copy-start(f32[1024]{0:T(1024)S(1)} %get-tuple-element.395) | copy-start | bytes 12292
  30.3 130.2 %copy-start.27 = (f32[768]{0:T(1024)}, f32[768]{0:T(1024)S(1)}, u32[]{:S(2)}) copy-start(f32[768]{0:T(1024)S(1)} %convert_element_type.283) | copy-start | bytes 9220
  72.2 5.7 copy-start.3
  160.5 9.1 %copy-start.31 = (f32[1024]{0:T(1024)}, f32[1024]{0:T(1024)S(1)}, u32[]{:S(2)}) copy-start(f32[1024]{0:T(1024)S(1)} %multiply_reduce_fusion.3) | copy-start | bytes 12292
  161.7 7.8 %copy-start.29 = (f32[1024]{0:T(1024)}, f32[1024]{0:T(1024)S(1)}, u32[]{:S(2)}) copy-start(f32[1024]{0:T(1024)S(1)} %fusion.115) | copy-start | bytes 12292
  162.2 23.8 %copy-start.13 = (bf16[1024,768]{0,1:T(8,128)(2,1)}, bf16[1024,768]{0,1:T(8,128)(2,1)S(1)}, u32[]{:S(2)}) copy-start(bf16[1024,768]{0,1:T(8,128)(2,1)S(1)} %fusion.101) | copy-start | bytes 4718596
  181.1 4.9 copy-start.8
  181.1 4.9 copy-start.40
  181.1 38.6 %slice-start = ((s8[4718592]{0:T(1024)(128)(4,1)}), s8[524288]{0:T(1024)(128)(4,1)S(1)}, s32[]{:S(2)}) async-start(s8[4718592]{0:T(1024)(128)(4,1)} %bitcast.396), calls=%async_computation.14 | async-start | bytes 1048576
  186.0 33.7 %copy-start.1 = (f32[1024,768]{0,1:T(8,128)S(1)}, f32[1024,768]{0,1:T(8,128)}, u32[]{:S(2)}) copy-start(f32[1024,768]{0,1:T(8,128)} %copy-done) | copy-start | bytes 9437188
  186.0 33.7 %slice-start.1 = ((s8[4718592]{0:T(1024)(128)(4,1)}), s8[4194304]{0:T(1024)(128)(4,1)S(1)}, s32[]{:S(2)}) async-start(s8[4718592]{0:T(1024)(128)(4,1)} %bitcast.396), calls=%async_computation.15 | async-start | bytes 8388608
  186.0 33.7 %copy-start.26 = (f32[1024]{0:T(1024)S(1)}, f32[1024]{0:T(1024)}, u32[]{:S(2)}) copy-start(f32[1024]{0:T(1024)} %copy-done.25) | copy-start | bytes 12292
  186.1 33.7 %copy-start.28 = (f32[768]{0:T(1024)S(1)}, f32[768]{0:T(1024)}, u32[]{:S(2)}) copy-start(f32[768]{0:T(1024)} %copy-done.27) | copy-start | bytes 9220
  186.1 33.7 %copy-start.30 = (f32[1024]{0:T(1024)S(1)}, f32[1024]{0:T(1024)}, u32[]{:S(2)}) copy-start(f32[1024]{0:T(1024)} %copy-done.29) | copy-start | bytes 12292
  186.1 33.7 %copy-start.39 = (f32[768]{0:T(1024)S(1)}, f32[768]{0:T(1024)}, u32[]{:S(2)}) copy-start(f32[768]{0:T(1024)} %convert_element_type.284) | copy-start | bytes 9220
  186.1 33.7 %copy-start.43 = (f32[768]{0:T(1024)S(1)}, f32[768]{0:T(1024)}, u32[]{:S(2)}) copy-start(f32[768]{0:T(1024)} %convert_element_type.288) | copy-start | bytes 9220
  219.7 5.4 copy-start.58
  219.8 5.3 copy-start.2
  219.8 5.3 copy-start.24
  247.8 11.2 %copy-start.32 = (f32[1024]{0:T(1024)S(1)}, f32[1024]{0:T(1024)}, u32[]{:S(2)}) copy-start(f32[1024]{0:T(1024)} %copy-done.31) | copy-start | bytes 12292
  268.2 207.8 %reduce-scatter.11.cloned.1.call-start = ((), (), s32[]{:S(2)}) async-start(), calls=%async_computation.8 | async-start | bytes 5898240 | tf_op jit(solution)/shard_map/reduce_scatter | solution.py:110
  284.0 191.9 %reduce-scatter.9.cloned.1.call-start = ((), (), s32[]{:S(2)}) async-start(), calls=%async_computation.7 | async-start | bytes 5898240 | tf_op jit(solution)/shard_map/reduce_scatter | solution.py:107
  323.9 6.7 copy-start.20
  330.6 5.7 copy-start.23
  336.4 180.5 %reduce-scatter.5.cloned.1.call-start = ((), (), s32[]{:S(2)}) async-start(), calls=%async_computation.4 | async-start | bytes 4423680 | tf_op jit(solution)/shard_map/reduce_scatter | solution.py:101
  336.9 118.5 %copy-start.34 = (f32[1024]{0:T(1024)S(1)}, f32[1024]{0:T(1024)}, u32[]{:S(2)}) copy-start(f32[1024]{0:T(1024)} %copy-done.33) | copy-start | bytes 12292
  336.9 118.5 %copy-start.36 = (f32[1024]{0:T(1024)S(1)}, f32[1024]{0:T(1024)}, u32[]{:S(2)}) copy-start(f32[1024]{0:T(1024)} %copy-done.35) | copy-start | bytes 12292
  455.4 6.3 copy-start.6
  475.8 44.7 %copy-start.57 = (bf16[192]{0:T(256)(128)(2,1)S(1)}, bf16[192]{0:T(256)(128)(2,1)}, u32[]{:S(2)}) copy-start(bf16[192]{0:T(256)(128)(2,1)} %param.32) | copy-start | bytes 1156
  475.9 162.6 %all-reduce.21.cloned.1.call-start = ((), (), s32[]{:S(2)}) async-start(), calls=%async_computation.13 | async-start | bytes 5308416 | tf_op jit(solution)/shard_map/psum | solution.py:141
  476.6 271.8 %all-gather.11.cloned.1.call-start = ((), (), s32[]{:S(2)}) async-start(), calls=%async_computation.5 | async-start | bytes 7962624 | tf_op jit(solution)/shard_map/all_gather | solution.py:140
  (23 other events, 61.3 us)
Sparse Core Ops, SparseCore 0:
  9.7 20.2 all-gather.14
  31.6 30.7 all-gather.12
  64.0 37.4 all-gather.18
  102.9 37.4 all-gather.16
  268.3 26.0 reduce-scatter.6
  297.0 47.7 reduce-scatter.10
  347.3 47.8 reduce-scatter.8
  476.0 40.8 reduce-scatter.4
  520.9 117.5 all-reduce.20
  640.5 107.7 all-gather.10
